TPU v7x, 32 devices: a whole 2x2x4 slice. The times are simulated.
32 devices in a mesh: groups: 2 (over y), space: 8 (over z, x), tm: 2 (over core).
Axes of the slice: x: 2, y: 2, z: 4, core: 2. Of those that a mesh axis runs over, the one named last changes fastest.
Arguments:
- base_latent: bfloat16 [64, 2, 12, 128], P(('groups', 'space'), 'tm'), parts along dimension 0, may hold values from -6 to 6
- cotangent: bfloat16 [64, 8, 48, 128], P(('groups', 'space'), 'tm'), parts along dimension 0, may hold values from -6 to 6
- w_spatial: bfloat16 [3, 3, 128, 128], replicated, may hold values from -0.1875 to 0.1875
- w_temporal: bfloat16 [5, 128, 128], replicated, may hold values from -0.25 to 0.25
Outputs:
- result: bfloat16 [64, 8, 48, 128], P(('groups', 'space'), 'tm'), parts along dimension 0
- grad_base: float32 [64, 2, 12, 128], P(('groups', 'space'), 'tm'), parts along dimension 0
- grad_spatial: float32 [6, 3, 128, 128], P('groups'), parts along dimension 0
- grad_temporal: float32 [10, 128, 128], P('groups'), parts along dimension 0
There are 2 independent parts, one for each index of `groups`. A program takes and returns all parts, laid end to end along the dimension named above; an argument that names none is the same for every part. Nothing has to cross between parts.
All inputs are finite; a program needn't handle non-finite values.
Results may differ from a plain program's by a relative error of at most 0.0064.
Values may be sent and summed in bfloat16 or wider, within the bound.
No kernel may reach another device: no remote copies, remote signals or barrier semaphores. Data moves between devices by JAX's collectives and lax.ppermute only.
A program may use at most 64 MiB of HBM per device.

v0:
```python
import jax
import jax.numpy as jnp
from jax import lax
from jax.sharding import PartitionSpec as P

FRAME_DILATION = 2


def shifted(value, axis, by):
    count = lax.axis_size(axis)
    pairs = [(i, i + by) for i in range(count) if 0 <= i + by < count]
    return lax.ppermute(value, axis, pairs)


def extended(cells, sides, width):
    for axis, dim in sides:
        count = lax.axis_size(axis)
        ends = count - 1
        head = lax.slice_in_dim(cells, 0, width, axis=dim)
        tail = lax.slice_in_dim(cells, cells.shape[dim] - width, cells.shape[dim], axis=dim)
        cells = jnp.concatenate(
            [
                lax.ppermute(tail, axis, [(i, (i + 1) % count) for i in range(ends)]),
                cells,
                lax.ppermute(head, axis, [((i + 1) % count, i) for i in range(ends)]),
            ],
            axis=dim,
        )
    return cells


def widen_cols(field):
    left_cols = jnp.concatenate([field[:, :, :1], field[:, :, :-1]], axis=2)
    right_cols = jnp.concatenate([field[:, :, 1:], field[:, :, -1:]], axis=2)
    phases = jnp.stack(
        [
            0.375 * left_cols + 0.625 * field,
            0.125 * left_cols + 0.875 * field,
            0.875 * field + 0.125 * right_cols,
            0.625 * field + 0.375 * right_cols,
        ],
        axis=3,
    )
    return phases.reshape(field.shape[0], field.shape[1], field.shape[2] * 4, field.shape[3])


def widen_rows(below_rows, middle, above_rows):
    phases = jnp.stack(
        [
            0.375 * below_rows + 0.625 * middle,
            0.125 * below_rows + 0.875 * middle,
            0.875 * middle + 0.125 * above_rows,
            0.625 * middle + 0.375 * above_rows,
        ],
        axis=2,
    )
    return phases.reshape(middle.shape[0], middle.shape[1] * 4, middle.shape[2], middle.shape[3])


def silu_slope(value):
    sigmoid_val = jax.nn.sigmoid(value)
    return sigmoid_val * (1.0 + value * (1.0 - sigmoid_val))


def conv_three(padded, weight, row_count, col_count, start):
    frame_count = padded.shape[0]
    channels = weight.shape[3]
    summed = jnp.zeros((frame_count * row_count * col_count, channels), jnp.float32)
    for tap_row in range(3):
        for tap_col in range(3):
            r0 = start - tap_row if start else tap_row
            c0 = start - tap_col if start else tap_col
            frame_window = padded[:, r0 : r0 + row_count, c0 : c0 + col_count].reshape(
                -1, padded.shape[3]
            )
            kernel = weight[tap_row, tap_col] if not start else weight[tap_row, tap_col].T
            summed = summed + jnp.dot(frame_window, kernel, preferred_element_type=jnp.float32)
    return summed.reshape(frame_count, row_count, col_count, channels)


def space_grads(padded, delta, row_count, col_count):
    flat = delta.reshape(-1, delta.shape[3])
    taps = []
    for tap_row in range(3):
        for tap_col in range(3):
            frame_window = padded[
                :, tap_row : tap_row + row_count, tap_col : tap_col + col_count
            ].reshape(-1, padded.shape[3])
            taps.append(
                lax.dot_general(
                    frame_window, flat, (((0,), (0,)), ((), ())), preferred_element_type=jnp.float32
                )
            )
    return jnp.stack(taps).reshape(3, 3, padded.shape[3], delta.shape[3])


def conv_time(frames_extended, weight, frame_count, reversed_order):
    channels = weight.shape[2]
    tensor_shape = frames_extended.shape
    summed = jnp.zeros((frame_count * tensor_shape[1] * tensor_shape[2], channels), jnp.float32)
    for kernel_tap in range(5):
        frame_offset = (
            (4 - kernel_tap) * FRAME_DILATION if reversed_order else kernel_tap * FRAME_DILATION
        )
        frame_window = frames_extended[frame_offset : frame_offset + frame_count].reshape(
            -1, tensor_shape[3]
        )
        kernel = weight[kernel_tap].T if reversed_order else weight[kernel_tap]
        summed = summed + jnp.dot(frame_window, kernel, preferred_element_type=jnp.float32)
    return summed.reshape(frame_count, tensor_shape[1], tensor_shape[2], channels)


def time_grads(frames_extended, delta, frame_count):
    flat = delta.reshape(-1, delta.shape[3])
    taps = []
    for kernel_tap in range(5):
        frame_window = frames_extended[
            kernel_tap * FRAME_DILATION : kernel_tap * FRAME_DILATION + frame_count
        ].reshape(-1, frames_extended.shape[3])
        taps.append(
            lax.dot_general(
                frame_window, flat, (((0,), (0,)), ((), ())), preferred_element_type=jnp.float32
            )
        )
    return jnp.stack(taps)


def shrink_base(grad_image, row_rank, row_devices, latent_shape):
    frame_count, low_rows, low_cols, channels = latent_shape
    _, col_pull = jax.vjp(
        widen_cols, jnp.zeros((frame_count, grad_image.shape[1], low_cols, channels), jnp.float32)
    )
    narrow = col_pull(grad_image)[0].reshape(frame_count, low_rows, 4, low_cols, channels)
    to_lower = 0.375 * narrow[:, :, 0] + 0.125 * narrow[:, :, 1]
    to_middle = (
        0.625 * narrow[:, :, 0]
        + 0.875 * narrow[:, :, 1]
        + 0.875 * narrow[:, :, 2]
        + 0.625 * narrow[:, :, 3]
    )
    to_upper = 0.125 * narrow[:, :, 2] + 0.375 * narrow[:, :, 3]
    from_above = shifted(to_lower, "tm", -1)
    from_below = shifted(to_upper, "tm", 1)
    next_lower = jnp.concatenate([to_lower[:, 1:], from_above], axis=1)
    prev_upper = jnp.concatenate([from_below, to_upper[:, :-1]], axis=1)
    edge_low = jnp.where(row_rank == 0, to_lower, jnp.zeros_like(to_lower))
    edge_high = jnp.where(row_rank == row_devices - 1, to_upper, jnp.zeros_like(to_upper))
    empty_rows = jnp.zeros((frame_count, low_rows - 1, low_cols, channels), jnp.float32)
    summed = to_middle + next_lower + prev_upper
    return (
        summed
        + jnp.concatenate([edge_low, empty_rows], axis=1)
        + jnp.concatenate([empty_rows, edge_high], axis=1)
    )


def local(base_latent, cotangent, w_spatial, w_temporal):
    row_rank = lax.axis_index("tm")
    row_devices = lax.axis_size("tm")
    padded_base = extended(base_latent, (("tm", 1),), 1)
    low_first = jnp.where(row_rank == 0, base_latent, padded_base[:, :1])
    high_last = jnp.where(row_rank == row_devices - 1, base_latent, padded_base[:, -1:])
    latent32 = base_latent.astype(jnp.float32)
    below_rows = jnp.concatenate([low_first, base_latent[:, :-1]], axis=1).astype(jnp.float32)
    above_rows = jnp.concatenate([base_latent[:, 1:], high_last], axis=1).astype(jnp.float32)
    upsampled = widen_cols(widen_rows(below_rows, latent32, above_rows)).astype(jnp.bfloat16)
    frame_count, row_count, col_count = (upsampled.shape[0], upsampled.shape[1], upsampled.shape[2])
    image_ext = extended(upsampled, (("tm", 1),), 1)
    padded = jnp.pad(image_ext, ((0, 0), (0, 0), (1, 1), (0, 0)))
    pre_one = conv_three(padded, w_spatial, row_count, col_count, 0)
    first_activation = jax.nn.silu(pre_one).astype(jnp.bfloat16)
    frames_extended = extended(first_activation, (("space", 0),), 2 * FRAME_DILATION)
    pre_two = conv_time(frames_extended, w_temporal, frame_count, False)
    result = (upsampled.astype(jnp.float32) + jax.nn.silu(pre_two)).astype(jnp.bfloat16)
    upstream = cotangent.astype(jnp.float32)
    second_gradient = (upstream * silu_slope(pre_two)).astype(jnp.bfloat16)
    temporal_local = time_grads(frames_extended, second_gradient, frame_count)
    grad_temporal = lax.psum(temporal_local, ("space", "tm"))
    gradient_extended = extended(second_gradient, (("space", 0),), 2 * FRAME_DILATION)
    back_one = conv_time(gradient_extended, w_temporal, frame_count, True)
    delta_one = (back_one * silu_slope(pre_one)).astype(jnp.bfloat16)
    spatial_local = space_grads(padded, delta_one, row_count, col_count)
    delta_rows = extended(delta_one, (("tm", 1),), 1)
    delta_pad = jnp.pad(delta_rows, ((0, 0), (0, 0), (1, 1), (0, 0)))
    grad_image = upstream + conv_three(delta_pad, w_spatial, row_count, col_count, 2)
    grad_base = shrink_base(grad_image, row_rank, row_devices, base_latent.shape)
    grad_spatial = lax.psum(spatial_local, ("space", "tm"))
    return (result, grad_base, grad_spatial, grad_temporal)


def solution(mesh):
    in_specs = (
        P(("groups", "space"), "tm", None, None),
        P(("groups", "space"), "tm", None, None),
        P(),
        P(),
    )
    out_specs = (
        P(("groups", "space"), "tm", None, None),
        P(("groups", "space"), "tm", None, None),
        P("groups", None, None, None),
        P("groups", None, None),
    )
    return jax.shard_map(local, mesh=mesh, in_specs=in_specs, out_specs=out_specs, check_vma=False)
```

profile of v0, /device:TPU:0, one launch (start us, length us, event | category | flops | bytes accessed | tf_op | source)
XLA Modules:
  0.0 162.9 jit_solution(3683068652345166377)
XLA Ops:
  7.2 0.8 copy.55
  8.0 2.4 %collective-permute-start = (bf16[4,1,12,128]{3,1,2,0:T(2,128)(2,1)S(1)}, bf16[4,1,12,128]{3,1,2,0:T(2,128)(2,1)S(1)}, u32[]{:S(2)}, u32[]{:S(2)}) collective-permute-start(bf16[4,1,12,128]{3,1,2,0:T(2,128)(2,1)S(1)} %copy.55), channel_id=1, source_target_pairs={{0,1},{2,3},{4,5},{6,7},{8,9},{10,11},{12,13},{14,15},{16,17},{18,... | collective-permute-start | bytes 36872 | tf_op jit(solution)/shard_map/ppermute | solution.py:23
  10.4 1.3 collective-permute-start.1
  11.7 1.8 %collective-permute-done.1 = bf16[4,1,12,128]{3,1,2,0:T(2,128)(2,1)S(1)} collective-permute-done((bf16[4,1,12,128]{3,1,2,0:T(2,128)(2,1)S(1)}, bf16[4,1,12,128]{3,1,2,0:T(2,128)(2,1)S(1)}, u32[]{:S(2)}, u32[]{:S(2)}) %collective-permute-start.1) | collective-permute-done | bytes 12320 | tf_op jit(solution)/shard_map/ppermute | solution.py:25
  14.4 2.1 %collective-permute-start.2 = (bf16[4,1,48,128]{3,2,1,0:T(8,128)(2,1)S(1)}, bf16[4,1,48,128]{3,2,1,0:T(8,128)(2,1)S(1)}, u32[]{:S(2)}, u32[]{:S(2)}) collective-permute-start(bf16[4,1,48,128]{3,2,1,0:T(8,128)(2,1)S(1)} %get-tuple-element.34), channel_id=1, source_target_pairs={{0,1},{2,3},{4,5},{6,7},{8,9},{10,11},{12,13},{14,15},{16,17},{18,... | collective-permute-start | bytes 147464 | tf_op jit(solution)/shard_map/ppermute | solution.py:23
  16.5 1.3 collective-permute-start.3
  17.8 1.8 %collective-permute-done.3 = bf16[4,1,48,128]{3,2,1,0:T(8,128)(2,1)S(1)} collective-permute-done((bf16[4,1,48,128]{3,2,1,0:T(8,128)(2,1)S(1)}, bf16[4,1,48,128]{3,2,1,0:T(8,128)(2,1)S(1)}, u32[]{:S(2)}, u32[]{:S(2)}) %collective-permute-start.3) | collective-permute-done | bytes 49184 | tf_op jit(solution)/shard_map/ppermute | solution.py:25
  19.9 0.8 copy-done
  22.7 4.2 %collective-permute-start.4 = (bf16[4,4,48,128]{3,2,1,0:T(8,128)(2,1)S(1)}, bf16[4,4,48,128]{3,2,1,0:T(8,128)(2,1)S(1)}, u32[]{:S(2)}, u32[]{:S(2)}) collective-permute-start(bf16[4,4,48,128]{3,2,1,0:T(8,128)(2,1)S(1)} %multiply_convert_fusion.3), channel_id=1, source_target_pairs={{0,2},{2,4},{4,6},{6,8},{8,10},{10,12},{12,14},{1,3},{3,5},{5,7},{... | collective-permute-start | bytes 589832 | tf_op jit(solution)/shard_map/ppermute | solution.py:23
  26.9 1.3 collective-permute-start.5
  28.4 3.0 %collective-permute-done.4 = bf16[4,4,48,128]{3,2,1,0:T(8,128)(2,1)S(1)} collective-permute-done((bf16[4,4,48,128]{3,2,1,0:T(8,128)(2,1)S(1)}, bf16[4,4,48,128]{3,2,1,0:T(8,128)(2,1)S(1)}, u32[]{:S(2)}, u32[]{:S(2)}) %collective-permute-start.4) | collective-permute-done | bytes 196640 | tf_op jit(solution)/shard_map/ppermute | solution.py:23
  31.4 4.0 %collective-permute-done.5 = bf16[4,4,48,128]{3,2,1,0:T(8,128)(2,1)S(1)} collective-permute-done((bf16[4,4,48,128]{3,2,1,0:T(8,128)(2,1)S(1)}, bf16[4,4,48,128]{3,2,1,0:T(8,128)(2,1)S(1)}, u32[]{:S(2)}, u32[]{:S(2)}) %collective-permute-start.5) | collective-permute-done | bytes 196640 | tf_op jit(solution)/shard_map/ppermute | solution.py:25
  37.0 0.9 fusion.21
  37.9 1.3 collective-permute-start.6
  39.2 5.1 %collective-permute-start.7 = (bf16[4,4,48,128]{3,2,1,0:T(8,128)(2,1)S(1)}, bf16[4,4,48,128]{3,2,1,0:T(8,128)(2,1)S(1)}, u32[]{:S(2)}, u32[]{:S(2)}) collective-permute-start(bf16[4,4,48,128]{3,2,1,0:T(8,128)(2,1)S(1)} %get-tuple-element.10), channel_id=1, source_target_pairs={{0,2},{2,4},{4,6},{6,8},{8,10},{10,12},{12,14},{1,3},{3,5},{5,7},{... | collective-permute-start | bytes 589832 | tf_op jit(solution)/shard_map/ppermute | solution.py:23
  46.5 5.2 %collective-permute-done.7 = bf16[4,4,48,128]{3,2,1,0:T(8,128)(2,1)S(1)} collective-permute-done((bf16[4,4,48,128]{3,2,1,0:T(8,128)(2,1)S(1)}, bf16[4,4,48,128]{3,2,1,0:T(8,128)(2,1)S(1)}, u32[]{:S(2)}, u32[]{:S(2)}) %collective-permute-start.7) | collective-permute-done | bytes 196640 | tf_op jit(solution)/shard_map/ppermute | solution.py:23
  54.6 1.9 %collective-permute-start.8 = (bf16[4,1,48,128]{3,2,1,0:T(8,128)(2,1)S(1)}, bf16[4,1,48,128]{3,2,1,0:T(8,128)(2,1)S(1)}, u32[]{:S(2)}, u32[]{:S(2)}) collective-permute-start(bf16[4,1,48,128]{3,2,1,0:T(8,128)(2,1)S(1)} %get-tuple-element.26), channel_id=1, source_target_pairs={{0,1},{2,3},{4,5},{6,7},{8,9},{10,11},{12,13},{14,15},{16,17},{18,... | collective-permute-start | bytes 147464 | tf_op jit(solution)/shard_map/ppermute | solution.py:23
  56.6 1.3 collective-permute-start.9
  58.4 0.8 copy-done.2
  63.3 1.3 collective-permute-start.10
  64.6 3.0 %collective-permute-start.11 = (f32[4,1,12,128]{3,1,2,0:T(1,128)S(1)}, f32[4,1,12,128]{3,1,2,0:T(1,128)S(1)}, u32[]{:S(2)}, u32[]{:S(2)}) collective-permute-start(f32[4,1,12,128]{3,1,2,0:T(1,128)S(1)} %get-tuple-element.40), channel_id=1, source_target_pairs={{0,1},{2,3},{4,5},{6,7},{8,9},{10,11},{12,13},{14,15},{16,17},{18,... | collective-permute-start | bytes 73736 | tf_op jit(solution)/shard_map/ppermute | solution.py:12
  67.7 0.8 collective-permute-done.11
  69.2 84.1 %all-reduce.8.cloned.1.call-done = (f32[3,3,128,128]{3,2,1,0:T(8,128)}, f32[5,128,128]{2,1,0:T(8,128)}) async-done(((f32[3,3,128,128]{3,2,1,0:T(8,128)}, f32[5,128,128]{2,1,0:T(8,128)}), (f32[3,3,128,128]{3,2,1,0:T(8,128)}, f32[5,128,128]{2,1,0:T(8,128)})) %all-reduce.8.cloned.1.call-update) | async-done | bytes 917520 | tf_op jit(solution)/shard_map/psum | solution.py:187
  153.4 2.0 %copy.127 = f32[3,3,128,128]{3,2,1,0:T(8,128)} copy(f32[3,3,128,128]{3,2,1,0:T(8,128)} %get-tuple-element.58) | data formatting | bytes 1179648
  (94 shorter events, 15.8 us)
Async XLA Ops:
  7.2 146.2 %all-reduce.8.cloned.1.call-start = ((), (), s32[]{:S(2)}) async-start(), calls=%async_computation | async-start | bytes 1835008 | tf_op jit(solution)/shard_map/psum | solution.py:187
  7.2 6.3 %copy-start.6 = (bf16[4,1,12,128]{3,0,2,1:T(4,128)(2,1)S(1)}, bf16[4,1,12,128]{3,0,2,1:T(4,128)(2,1)}, u32[]{:S(2)}) copy-start(bf16[4,1,12,128]{3,0,2,1:T(4,128)(2,1)} %param.4) | copy-start | bytes 36868
  8.0 3.7 %collective-permute-start = (bf16[4,1,12,128]{3,1,2,0:T(2,128)(2,1)S(1)}, bf16[4,1,12,128]{3,1,2,0:T(2,128)(2,1)S(1)}, u32[]{:S(2)}, u32[]{:S(2)}) collective-permute-start(bf16[4,1,12,128]{3,1,2,0:T(2,128)(2,1)S(1)} %copy.55), channel_id=1, source_target_pairs={{0,1},{2,3},{4,5},{6,7},{8,9},{10,11},{12,13},{14,15},{16,17},{18,... | collective-permute-start | bytes 36872 | tf_op jit(solution)/shard_map/ppermute | solution.py:23
  10.4 3.1 %collective-permute-start.1 = (bf16[4,1,12,128]{3,1,2,0:T(2,128)(2,1)S(1)}, bf16[4,1,12,128]{3,1,2,0:T(2,128)(2,1)S(1)}, u32[]{:S(2)}, u32[]{:S(2)}) collective-permute-start(bf16[4,1,12,128]{3,1,2,0:T(2,128)(2,1)S(1)} %copy.55), channel_id=1, source_target_pairs={{1,0},{3,2},{5,4},{7,6},{9,8},{11,10},{13,12},{15,14},{17,16},{19,... | collective-permute-start | bytes 36872 | tf_op jit(solution)/shard_map/ppermute | solution.py:25
  14.4 3.4 %collective-permute-start.2 = (bf16[4,1,48,128]{3,2,1,0:T(8,128)(2,1)S(1)}, bf16[4,1,48,128]{3,2,1,0:T(8,128)(2,1)S(1)}, u32[]{:S(2)}, u32[]{:S(2)}) collective-permute-start(bf16[4,1,48,128]{3,2,1,0:T(8,128)(2,1)S(1)} %get-tuple-element.34), channel_id=1, source_target_pairs={{0,1},{2,3},{4,5},{6,7},{8,9},{10,11},{12,13},{14,15},{16,17},{18,... | collective-permute-start | bytes 147464 | tf_op jit(solution)/shard_map/ppermute | solution.py:23
  16.5 3.1 %collective-permute-start.3 = (bf16[4,1,48,128]{3,2,1,0:T(8,128)(2,1)S(1)}, bf16[4,1,48,128]{3,2,1,0:T(8,128)(2,1)S(1)}, u32[]{:S(2)}, u32[]{:S(2)}) collective-permute-start(bf16[4,1,48,128]{3,2,1,0:T(8,128)(2,1)S(1)} %get-tuple-element.35), channel_id=1, source_target_pairs={{1,0},{3,2},{5,4},{7,6},{9,8},{11,10},{13,12},{15,14},{17,16},{19,... | collective-permute-start | bytes 147464 | tf_op jit(solution)/shard_map/ppermute | solution.py:25
  19.7 1.0 copy-start
  22.5 5.7 %copy-start.3 = (bf16[5,128,128]{2,1,0:T(8,128)(2,1)S(1)}, bf16[5,128,128]{2,1,0:T(8,128)(2,1)}, u32[]{:S(2)}) copy-start(bf16[5,128,128]{2,1,0:T(8,128)(2,1)} %param.7) | copy-start | bytes 491524
  22.7 8.8 %collective-permute-start.4 = (bf16[4,4,48,128]{3,2,1,0:T(8,128)(2,1)S(1)}, bf16[4,4,48,128]{3,2,1,0:T(8,128)(2,1)S(1)}, u32[]{:S(2)}, u32[]{:S(2)}) collective-permute-start(bf16[4,4,48,128]{3,2,1,0:T(8,128)(2,1)S(1)} %multiply_convert_fusion.3), channel_id=1, source_target_pairs={{0,2},{2,4},{4,6},{6,8},{8,10},{10,12},{12,14},{1,3},{3,5},{5,7},{... | collective-permute-start | bytes 589832 | tf_op jit(solution)/shard_map/ppermute | solution.py:23
  26.9 8.6 %collective-permute-start.5 = (bf16[4,4,48,128]{3,2,1,0:T(8,128)(2,1)S(1)}, bf16[4,4,48,128]{3,2,1,0:T(8,128)(2,1)S(1)}, u32[]{:S(2)}, u32[]{:S(2)}) collective-permute-start(bf16[4,4,48,128]{3,2,1,0:T(8,128)(2,1)S(1)} %multiply_convert_fusion.3), channel_id=1, source_target_pairs={{2,0},{4,2},{6,4},{8,6},{10,8},{12,10},{14,12},{3,1},{5,3},{7,5},{... | collective-permute-start | bytes 589832 | tf_op jit(solution)/shard_map/ppermute | solution.py:25
  36.1 0.9 copy-start.1
  37.9 8.5 %collective-permute-start.6 = (bf16[4,4,48,128]{3,2,1,0:T(8,128)(2,1)S(1)}, bf16[4,4,48,128]{3,2,1,0:T(8,128)(2,1)S(1)}, u32[]{:S(2)}, u32[]{:S(2)}) collective-permute-start(bf16[4,4,48,128]{3,2,1,0:T(8,128)(2,1)S(1)} %get-tuple-element.10), channel_id=1, source_target_pairs={{2,0},{4,2},{6,4},{8,6},{10,8},{12,10},{14,12},{3,1},{5,3},{7,5},{... | collective-permute-start | bytes 589832 | tf_op jit(solution)/shard_map/ppermute | solution.py:25
  39.2 12.4 %collective-permute-start.7 = (bf16[4,4,48,128]{3,2,1,0:T(8,128)(2,1)S(1)}, bf16[4,4,48,128]{3,2,1,0:T(8,128)(2,1)S(1)}, u32[]{:S(2)}, u32[]{:S(2)}) collective-permute-start(bf16[4,4,48,128]{3,2,1,0:T(8,128)(2,1)S(1)} %get-tuple-element.10), channel_id=1, source_target_pairs={{0,2},{2,4},{4,6},{6,8},{8,10},{10,12},{12,14},{1,3},{3,5},{5,7},{... | collective-permute-start | bytes 589832 | tf_op jit(solution)/shard_map/ppermute | solution.py:23
  45.9 5.8 %copy-start.4 = (f32[5,128,128]{2,1,0:T(8,128)}, f32[5,128,128]{2,1,0:T(8,128)S(1)}, u32[]{:S(2)}) copy-start(f32[5,128,128]{2,1,0:T(8,128)S(1)} %fusion.10) | copy-start | bytes 983044
  54.6 4.6 %collective-permute-start.8 = (bf16[4,1,48,128]{3,2,1,0:T(8,128)(2,1)S(1)}, bf16[4,1,48,128]{3,2,1,0:T(8,128)(2,1)S(1)}, u32[]{:S(2)}, u32[]{:S(2)}) collective-permute-start(bf16[4,1,48,128]{3,2,1,0:T(8,128)(2,1)S(1)} %get-tuple-element.26), channel_id=1, source_target_pairs={{0,1},{2,3},{4,5},{6,7},{8,9},{10,11},{12,13},{14,15},{16,17},{18,... | collective-permute-start | bytes 147464 | tf_op jit(solution)/shard_map/ppermute | solution.py:23
  56.6 3.1 %collective-permute-start.9 = (bf16[4,1,48,128]{3,2,1,0:T(8,128)(2,1)S(1)}, bf16[4,1,48,128]{3,2,1,0:T(8,128)(2,1)S(1)}, u32[]{:S(2)}, u32[]{:S(2)}) collective-permute-start(bf16[4,1,48,128]{3,2,1,0:T(8,128)(2,1)S(1)} %get-tuple-element.27), channel_id=1, source_target_pairs={{1,0},{3,2},{5,4},{7,6},{9,8},{11,10},{13,12},{15,14},{17,16},{19,... | collective-permute-start | bytes 147464 | tf_op jit(solution)/shard_map/ppermute | solution.py:25
  58.4 0.8 copy-start.2
  62.4 0.7 copy-start.7
  63.3 4.3 %collective-permute-start.10 = (f32[4,1,12,128]{3,1,2,0:T(1,128)S(1)}, f32[4,1,12,128]{3,1,2,0:T(1,128)S(1)}, u32[]{:S(2)}, u32[]{:S(2)}) collective-permute-start(f32[4,1,12,128]{3,1,2,0:T(1,128)S(1)} %get-tuple-element.41), channel_id=1, source_target_pairs={{1,0},{3,2},{5,4},{7,6},{9,8},{11,10},{13,12},{15,14},{17,16},{19,... | collective-permute-start | bytes 73736 | tf_op jit(solution)/shard_map/ppermute | solution.py:12
  64.6 3.9 %collective-permute-start.11 = (f32[4,1,12,128]{3,1,2,0:T(1,128)S(1)}, f32[4,1,12,128]{3,1,2,0:T(1,128)S(1)}, u32[]{:S(2)}, u32[]{:S(2)}) collective-permute-start(f32[4,1,12,128]{3,1,2,0:T(1,128)S(1)} %get-tuple-element.40), channel_id=1, source_target_pairs={{0,1},{2,3},{4,5},{6,7},{8,9},{10,11},{12,13},{14,15},{16,17},{18,... | collective-permute-start | bytes 73736 | tf_op jit(solution)/shard_map/ppermute | solution.py:12
  153.4 2.0 %copy-start.5 = (f32[5,128,128]{2,1,0:T(8,128)S(1)}, f32[5,128,128]{2,1,0:T(8,128)}, u32[]{:S(2)}) copy-start(f32[5,128,128]{2,1,0:T(8,128)} %get-tuple-element.59) | copy-start | bytes 983044
Sparse Core Ops, SparseCore 0:
  59.3 93.9 all-reduce.7
where the time goes:
time: 163 us
  waiting for transfers between devices  102 us (63%)
  starting transfers between devices  26.5 us (16%)
  between operations  14.7 us (9%)
  matrix products  9.25 us (6%)
  local copies, waits for them, and re-layouts  7.29 us (4%)
  other arithmetic  3.34 us (2%)
    psum x1, waiting for transfers between devices, local(): grad_spatial = lax.psum(spatial_local, ('space', 'tm'))  84.1 us
    ppermute x5, starting transfers between devices, extended(): lax.ppermute(tail, axis, [(i, (i + 1) % count) for i in range(ends)])  15.7 us
    ppermute x5, waiting for transfers between devices, extended(): lax.ppermute(head, axis, [((i + 1) % count, i) for i in range(ends)])  8.69 us
    ppermute x5, waiting for transfers between devices, extended(): lax.ppermute(tail, axis, [(i, (i + 1) % count) for i in range(ends)])  8.19 us
    ppermute x5, starting transfers between devices, extended(): lax.ppermute(head, axis, [((i + 1) % count, i) for i in range(ends)])  6.45 us
    unnamed x19, local copies, waits for them, and re-layouts  6.45 us
    ppermute x2, starting transfers between devices, shifted(): return lax.ppermute(value, axis, pairs)  4.32 us
    dot_general x18, matrix products, conv_three(): jnp.dot(frame_window, kernel, preferred_element_type=jnp.float32)  3.61 us
  transfers between devices with their start and end apart: 13, of which 9 were waited for; matrix products, arithmetic and copies ran while one was open for 4% of the time, Pallas kernels for 0%

commit v1 on v0

--- a/solution.py
+++ b/solution.py
@@ -184,7 +184,7 @@
     delta_pad = jnp.pad(delta_rows, ((0, 0), (0, 0), (1, 1), (0, 0)))
     grad_image = upstream + conv_three(delta_pad, w_spatial, row_count, col_count, 2)
     grad_base = shrink_base(grad_image, row_rank, row_devices, base_latent.shape)
-    grad_spatial = lax.psum(spatial_local, ("space", "tm"))
+    grad_spatial = lax.psum(lax.psum(spatial_local, "tm"), "space")
     return (result, grad_base, grad_spatial, grad_temporal)
 
 

time: 163 us -> 257 us (1.58)
  waiting for transfers between devices: 102 us -> 195 us
    psum x1 -> x3, waiting for transfers between devices: 84.1 us -> 177 us  [the longest x2 89.7 us: local(): grad_spatial = lax.psum(lax.psum(spatial_local, 'tm'), 'space')]
  transfers between devices with their start and end apart: 13 -> 15, of which waited for: 9 -> 11; matrix products, arithmetic and copies ran while one was open for 4% -> 2% of each run, Pallas kernels for 0% -> 0%
where the time goes in v1:
time: 257 us
  waiting for transfers between devices  195 us (76%)
  starting transfers between devices  26.6 us (10%)
  between operations  14.4 us (6%)
  matrix products  9.25 us (4%)
  local copies, waits for them, and re-layouts  8 us (3%)
  other arithmetic  3.36 us (1%)
    psum x2, waiting for transfers between devices, local(): grad_spatial = lax.psum(lax.psum(spatial_local, 'tm'), 'space')  89.7 us
    psum x1, waiting for transfers between devices, local(): grad_temporal = lax.psum(temporal_local, ('space', 'tm'))  87.1 us
    ppermute x5, starting transfers between devices, extended(): lax.ppermute(tail, axis, [(i, (i + 1) % count) for i in range(ends)])  15.7 us
    ppermute x5, waiting for transfers between devices, extended(): lax.ppermute(head, axis, [((i + 1) % count, i) for i in range(ends)])  9.51 us
    ppermute x5, waiting for transfers between devices, extended(): lax.ppermute(tail, axis, [(i, (i + 1) % count) for i in range(ends)])  8.18 us
    unnamed x19, local copies, waits for them, and re-layouts  7.16 us
    ppermute x5, starting transfers between devices, extended(): lax.ppermute(head, axis, [((i + 1) % count, i) for i in range(ends)])  6.45 us
  transfers between devices with their start and end apart: 15, of which 11 were waited for; matrix products, arithmetic and copies ran while one was open for 2% of the time, Pallas kernels for 0%

profile of v1, /device:TPU:0, one launch (start us, length us, event | category | flops | bytes accessed | tf_op | source)
XLA Modules:
  0.0 257.0 jit_solution(4809223432138061681)
XLA Ops:
  8.0 2.4 collective-permute-start
  10.4 1.3 collective-permute-start.1
  11.7 1.8 collective-permute-done.1
  14.4 2.1 collective-permute-start.2
  16.5 1.3 collective-permute-start.3
  17.8 1.8 collective-permute-done.3
  22.7 4.2 %collective-permute-start.4 = (bf16[4,4,48,128]{3,2,1,0:T(8,128)(2,1)S(1)}, bf16[4,4,48,128]{3,2,1,0:T(8,128)(2,1)S(1)}, u32[]{:S(2)}, u32[]{:S(2)}) collective-permute-start(bf16[4,4,48,128]{3,2,1,0:T(8,128)(2,1)S(1)} %multiply_convert_fusion.3), channel_id=1, source_target_pairs={{0,2},{2,4},{4,6},{6,8},{8,10},{10,12},{12,14},{1,3},{3,5},{5,7},{... | collective-permute-start | bytes 589832 | tf_op jit(solution)/shard_map/ppermute | solution.py:23
  26.9 1.3 collective-permute-start.5
  28.4 3.0 %collective-permute-done.4 = bf16[4,4,48,128]{3,2,1,0:T(8,128)(2,1)S(1)} collective-permute-done((bf16[4,4,48,128]{3,2,1,0:T(8,128)(2,1)S(1)}, bf16[4,4,48,128]{3,2,1,0:T(8,128)(2,1)S(1)}, u32[]{:S(2)}, u32[]{:S(2)}) %collective-permute-start.4) | collective-permute-done | bytes 196640 | tf_op jit(solution)/shard_map/ppermute | solution.py:23
  31.4 4.0 %collective-permute-done.5 = bf16[4,4,48,128]{3,2,1,0:T(8,128)(2,1)S(1)} collective-permute-done((bf16[4,4,48,128]{3,2,1,0:T(8,128)(2,1)S(1)}, bf16[4,4,48,128]{3,2,1,0:T(8,128)(2,1)S(1)}, u32[]{:S(2)}, u32[]{:S(2)}) %collective-permute-start.5) | collective-permute-done | bytes 196640 | tf_op jit(solution)/shard_map/ppermute | solution.py:25
  37.1 0.9 fusion.21
  38.0 1.3 collective-permute-start.6
  39.2 5.1 %collective-permute-start.7 = (bf16[4,4,48,128]{3,2,1,0:T(8,128)(2,1)S(1)}, bf16[4,4,48,128]{3,2,1,0:T(8,128)(2,1)S(1)}, u32[]{:S(2)}, u32[]{:S(2)}) collective-permute-start(bf16[4,4,48,128]{3,2,1,0:T(8,128)(2,1)S(1)} %get-tuple-element.8), channel_id=1, source_target_pairs={{0,2},{2,4},{4,6},{6,8},{8,10},{10,12},{12,14},{1,3},{3,5},{5,7},{... | collective-permute-start | bytes 589832 | tf_op jit(solution)/shard_map/ppermute | solution.py:23
  45.4 1.1 collective-permute-done.6
  46.5 5.2 %collective-permute-done.7 = bf16[4,4,48,128]{3,2,1,0:T(8,128)(2,1)S(1)} collective-permute-done((bf16[4,4,48,128]{3,2,1,0:T(8,128)(2,1)S(1)}, bf16[4,4,48,128]{3,2,1,0:T(8,128)(2,1)S(1)}, u32[]{:S(2)}, u32[]{:S(2)}) %collective-permute-start.7) | collective-permute-done | bytes 196640 | tf_op jit(solution)/shard_map/ppermute | solution.py:23
  56.3 1.9 collective-permute-start.8
  58.2 1.3 collective-permute-start.9
  64.1 12.4 %all-reduce.9.cloned.1.call-done = f32[3,3,128,128]{3,2,1,0:T(8,128)} async-done(((f32[3,3,128,128]{3,2,1,0:T(8,128)}), f32[3,3,128,128]{3,2,1,0:T(8,128)}) %all-reduce.9.cloned.1.call-update) | async-done | bytes 589840 | tf_op jit(solution)/shard_map/psum | solution.py:187
  77.4 1.3 collective-permute-start.10
  78.7 3.0 %collective-permute-start.11 = (f32[4,1,12,128]{3,1,2,0:T(1,128)S(1)}, f32[4,1,12,128]{3,1,2,0:T(1,128)S(1)}, u32[]{:S(2)}, u32[]{:S(2)}) collective-permute-start(f32[4,1,12,128]{3,1,2,0:T(1,128)S(1)} %get-tuple-element.38), channel_id=1, source_target_pairs={{0,1},{2,3},{4,5},{6,7},{8,9},{10,11},{12,13},{14,15},{16,17},{18,... | collective-permute-start | bytes 73736 | tf_op jit(solution)/shard_map/ppermute | solution.py:12
  81.7 0.8 collective-permute-done.11
  83.3 87.1 %all-reduce.13.cloned.1.call-done = f32[5,128,128]{2,1,0:T(8,128)} async-done(((f32[5,128,128]{2,1,0:T(8,128)}), f32[5,128,128]{2,1,0:T(8,128)}) %all-reduce.13.cloned.1.call-update) | async-done | bytes 327696 | tf_op jit(solution)/shard_map/psum | solution.py:178
  170.4 77.3 %all-reduce.11.cloned.1.call-done = f32[3,3,128,128]{3,2,1,0:T(8,128)} async-done(((f32[3,3,128,128]{3,2,1,0:T(8,128)}), f32[3,3,128,128]{3,2,1,0:T(8,128)}) %all-reduce.11.cloned.1.call-update) | async-done | bytes 589840 | tf_op jit(solution)/shard_map/psum | solution.py:187
  247.7 2.0 copy.128
  (100 shorter events, 18.7 us)
Async XLA Ops:
  7.2 69.3 %all-reduce.9.cloned.1.call-start = ((), (), s32[]{:S(2)}) async-start(), calls=%async_computation | async-start | bytes 1179648 | tf_op jit(solution)/shard_map/psum | solution.py:187
  7.2 6.3 %copy-start.6 = (bf16[4,1,12,128]{3,0,2,1:T(4,128)(2,1)S(1)}, bf16[4,1,12,128]{3,0,2,1:T(4,128)(2,1)}, u32[]{:S(2)}) copy-start(bf16[4,1,12,128]{3,0,2,1:T(4,128)(2,1)} %param.4) | copy-start | bytes 36868
  8.0 3.7 %collective-permute-start = (bf16[4,1,12,128]{3,1,2,0:T(2,128)(2,1)S(1)}, bf16[4,1,12,128]{3,1,2,0:T(2,128)(2,1)S(1)}, u32[]{:S(2)}, u32[]{:S(2)}) collective-permute-start(bf16[4,1,12,128]{3,1,2,0:T(2,128)(2,1)S(1)} %copy.55), channel_id=1, source_target_pairs={{0,1},{2,3},{4,5},{6,7},{8,9},{10,11},{12,13},{14,15},{16,17},{18,... | collective-permute-start | bytes 36872 | tf_op jit(solution)/shard_map/ppermute | solution.py:23
  10.4 3.1 %collective-permute-start.1 = (bf16[4,1,12,128]{3,1,2,0:T(2,128)(2,1)S(1)}, bf16[4,1,12,128]{3,1,2,0:T(2,128)(2,1)S(1)}, u32[]{:S(2)}, u32[]{:S(2)}) collective-permute-start(bf16[4,1,12,128]{3,1,2,0:T(2,128)(2,1)S(1)} %copy.55), channel_id=1, source_target_pairs={{1,0},{3,2},{5,4},{7,6},{9,8},{11,10},{13,12},{15,14},{17,16},{19,... | collective-permute-start | bytes 36872 | tf_op jit(solution)/shard_map/ppermute | solution.py:25
  14.4 3.4 %collective-permute-start.2 = (bf16[4,1,48,128]{3,2,1,0:T(8,128)(2,1)S(1)}, bf16[4,1,48,128]{3,2,1,0:T(8,128)(2,1)S(1)}, u32[]{:S(2)}, u32[]{:S(2)}) collective-permute-start(bf16[4,1,48,128]{3,2,1,0:T(8,128)(2,1)S(1)} %get-tuple-element.32), channel_id=1, source_target_pairs={{0,1},{2,3},{4,5},{6,7},{8,9},{10,11},{12,13},{14,15},{16,17},{18,... | collective-permute-start | bytes 147464 | tf_op jit(solution)/shard_map/ppermute | solution.py:23
  16.5 3.1 %collective-permute-start.3 = (bf16[4,1,48,128]{3,2,1,0:T(8,128)(2,1)S(1)}, bf16[4,1,48,128]{3,2,1,0:T(8,128)(2,1)S(1)}, u32[]{:S(2)}, u32[]{:S(2)}) collective-permute-start(bf16[4,1,48,128]{3,2,1,0:T(8,128)(2,1)S(1)} %get-tuple-element.33), channel_id=1, source_target_pairs={{1,0},{3,2},{5,4},{7,6},{9,8},{11,10},{13,12},{15,14},{17,16},{19,... | collective-permute-start | bytes 147464 | tf_op jit(solution)/shard_map/ppermute | solution.py:25
  19.7 1.0 copy-start
  22.5 5.7 %copy-start.3 = (bf16[5,128,128]{2,1,0:T(8,128)(2,1)S(1)}, bf16[5,128,128]{2,1,0:T(8,128)(2,1)}, u32[]{:S(2)}) copy-start(bf16[5,128,128]{2,1,0:T(8,128)(2,1)} %param.7) | copy-start | bytes 491524
  22.7 8.8 %collective-permute-start.4 = (bf16[4,4,48,128]{3,2,1,0:T(8,128)(2,1)S(1)}, bf16[4,4,48,128]{3,2,1,0:T(8,128)(2,1)S(1)}, u32[]{:S(2)}, u32[]{:S(2)}) collective-permute-start(bf16[4,4,48,128]{3,2,1,0:T(8,128)(2,1)S(1)} %multiply_convert_fusion.3), channel_id=1, source_target_pairs={{0,2},{2,4},{4,6},{6,8},{8,10},{10,12},{12,14},{1,3},{3,5},{5,7},{... | collective-permute-start | bytes 589832 | tf_op jit(solution)/shard_map/ppermute | solution.py:23
  26.9 8.6 %collective-permute-start.5 = (bf16[4,4,48,128]{3,2,1,0:T(8,128)(2,1)S(1)}, bf16[4,4,48,128]{3,2,1,0:T(8,128)(2,1)S(1)}, u32[]{:S(2)}, u32[]{:S(2)}) collective-permute-start(bf16[4,4,48,128]{3,2,1,0:T(8,128)(2,1)S(1)} %multiply_convert_fusion.3), channel_id=1, source_target_pairs={{2,0},{4,2},{6,4},{8,6},{10,8},{12,10},{14,12},{3,1},{5,3},{7,5},{... | collective-permute-start | bytes 589832 | tf_op jit(solution)/shard_map/ppermute | solution.py:25
  36.1 0.9 copy-start.1
  38.0 8.5 %collective-permute-start.6 = (bf16[4,4,48,128]{3,2,1,0:T(8,128)(2,1)S(1)}, bf16[4,4,48,128]{3,2,1,0:T(8,128)(2,1)S(1)}, u32[]{:S(2)}, u32[]{:S(2)}) collective-permute-start(bf16[4,4,48,128]{3,2,1,0:T(8,128)(2,1)S(1)} %get-tuple-element.8), channel_id=1, source_target_pairs={{2,0},{4,2},{6,4},{8,6},{10,8},{12,10},{14,12},{3,1},{5,3},{7,5},{... | collective-permute-start | bytes 589832 | tf_op jit(solution)/shard_map/ppermute | solution.py:25
  39.2 12.4 %collective-permute-start.7 = (bf16[4,4,48,128]{3,2,1,0:T(8,128)(2,1)S(1)}, bf16[4,4,48,128]{3,2,1,0:T(8,128)(2,1)S(1)}, u32[]{:S(2)}, u32[]{:S(2)}) collective-permute-start(bf16[4,4,48,128]{3,2,1,0:T(8,128)(2,1)S(1)} %get-tuple-element.8), channel_id=1, source_target_pairs={{0,2},{2,4},{4,6},{6,8},{8,10},{10,12},{12,14},{1,3},{3,5},{5,7},{... | collective-permute-start | bytes 589832 | tf_op jit(solution)/shard_map/ppermute | solution.py:23
  55.1 0.8 copy-start.2
  56.0 114.4 %all-reduce.13.cloned.1.call-start = ((), (), s32[]{:S(2)}) async-start(), calls=%async_computation.2 | async-start | bytes 655360 | tf_op jit(solution)/shard_map/psum | solution.py:178
  56.3 4.3 %collective-permute-start.8 = (bf16[4,1,48,128]{3,2,1,0:T(8,128)(2,1)S(1)}, bf16[4,1,48,128]{3,2,1,0:T(8,128)(2,1)S(1)}, u32[]{:S(2)}, u32[]{:S(2)}) collective-permute-start(bf16[4,1,48,128]{3,2,1,0:T(8,128)(2,1)S(1)} %get-tuple-element.24), channel_id=1, source_target_pairs={{0,1},{2,3},{4,5},{6,7},{8,9},{10,11},{12,13},{14,15},{16,17},{18,... | collective-permute-start | bytes 147464 | tf_op jit(solution)/shard_map/ppermute | solution.py:23
  58.2 3.1 %collective-permute-start.9 = (bf16[4,1,48,128]{3,2,1,0:T(8,128)(2,1)S(1)}, bf16[4,1,48,128]{3,2,1,0:T(8,128)(2,1)S(1)}, u32[]{:S(2)}, u32[]{:S(2)}) collective-permute-start(bf16[4,1,48,128]{3,2,1,0:T(8,128)(2,1)S(1)} %get-tuple-element.25), channel_id=1, source_target_pairs={{1,0},{3,2},{5,4},{7,6},{9,8},{11,10},{13,12},{15,14},{17,16},{19,... | collective-permute-start | bytes 147464 | tf_op jit(solution)/shard_map/ppermute | solution.py:25
  59.8 0.7 copy-start.5
  60.5 187.2 %all-reduce.11.cloned.1.call-start = ((), (), s32[]{:S(2)}) async-start(), calls=%async_computation.1 | async-start | bytes 1179648 | tf_op jit(solution)/shard_map/psum | solution.py:187
  76.5 0.7 copy-start.7
  77.4 4.3 %collective-permute-start.10 = (f32[4,1,12,128]{3,1,2,0:T(1,128)S(1)}, f32[4,1,12,128]{3,1,2,0:T(1,128)S(1)}, u32[]{:S(2)}, u32[]{:S(2)}) collective-permute-start(f32[4,1,12,128]{3,1,2,0:T(1,128)S(1)} %get-tuple-element.39), channel_id=1, source_target_pairs={{1,0},{3,2},{5,4},{7,6},{9,8},{11,10},{13,12},{15,14},{17,16},{19,... | collective-permute-start | bytes 73736 | tf_op jit(solution)/shard_map/ppermute | solution.py:12
  78.7 3.9 %collective-permute-start.11 = (f32[4,1,12,128]{3,1,2,0:T(1,128)S(1)}, f32[4,1,12,128]{3,1,2,0:T(1,128)S(1)}, u32[]{:S(2)}, u32[]{:S(2)}) collective-permute-start(f32[4,1,12,128]{3,1,2,0:T(1,128)S(1)} %get-tuple-element.38), channel_id=1, source_target_pairs={{0,1},{2,3},{4,5},{6,7},{8,9},{10,11},{12,13},{14,15},{16,17},{18,... | collective-permute-start | bytes 73736 | tf_op jit(solution)/shard_map/ppermute | solution.py:12
  247.7 2.0 copy-start.4
Sparse Core Ops, SparseCore 0:
  56.1 20.3 all-reduce.8
  80.8 89.5 all-reduce.12
  173.8 73.9 all-reduce.10
